TPU v7x, 32 devices: a whole 2x2x4 slice. The times are simulated.
32 devices in a mesh: groups: 2 (over x), view: 16 (over z, y, core).
Axes of the slice: x: 2, y: 2, z: 4, core: 2. Of those that a mesh axis runs over, the one named last changes fastest.
Arguments:
- query: bfloat16 [4096, 1024], P(('groups', 'view')), parts along dimension 0, may hold values from -28 to 28
- keys: bfloat16 [4096, 1024], P(('groups', 'view')), parts along dimension 0, may hold values from -6 to 6
- values: bfloat16 [4096, 1024], P(('groups', 'view')), parts along dimension 0, may hold values from -6 to 6
- grad_out: bfloat16 [4096, 1024], P(('groups', 'view')), parts along dimension 0, may hold values from -6 to 6
- margin: int32 [32, 4, 1, 1], P('groups'), parts along dimension 0, may hold values 0 or 1
Outputs:
- attended: bfloat16 [4096, 1024], P(('groups', 'view')), parts along dimension 0
- grad_query: bfloat16 [4096, 1024], P(('groups', 'view')), parts along dimension 0
- grad_key: bfloat16 [4096, 1024], P(('groups', 'view')), parts along dimension 0
- grad_value: bfloat16 [4096, 1024], P(('groups', 'view')), parts along dimension 0
There are 2 independent parts, one for each index of `groups`. A program takes and returns all parts, laid end to end along the dimension named above; each array names one. Nothing has to cross between parts.
All inputs are finite; a program needn't handle non-finite values.
Results may differ from a plain program's by a relative error of at most 0.033.
Values may be sent and summed in bfloat16 or wider, within the bound.
No kernel may reach another device: no remote copies, remote signals or barrier semaphores. Data moves between devices by JAX's collectives and lax.ppermute only.
A program may use at most 64 MiB of HBM per device.

v0:
```python
import math

import jax
import jax.numpy as jnp
from jax import lax
from jax.sharding import PartitionSpec as P

H = 8
BLK = 128
SPAN = 2


NEG_FILL = -1e30


def from_behind(block, axis, distance):
    devices = range(lax.axis_size(axis))
    route = [((i - distance) % len(devices), i) for i in devices]
    return lax.ppermute(block, axis, route)


def mask_spans_of(margin, image_index, reach):
    mask_row = lax.dynamic_index_in_dim(margin, image_index, 0, keepdims=False)
    filled = jnp.ones((1,) + mask_row.shape[1:], mask_row.dtype)
    return jnp.concatenate([mask_row[:reach], filled, mask_row[reach:]], axis=0)


def block_allowed(mask_spans, block_rows):
    span_count, block_count, _ = mask_spans.shape
    block_grid = jnp.transpose(mask_spans, (1, 0, 2)).reshape(block_count, span_count * block_count)
    return jnp.repeat(jnp.repeat(block_grid, block_rows, axis=0), block_rows, axis=1) > 0


def body(query, keys, values, grad_out, margin):
    tokens = query.shape[0]
    row_width = query.shape[1]
    head_dim = row_width // H
    score_scale = 1.0 / math.sqrt(head_dim)
    position = lax.axis_index("view")
    key_value = jnp.stack((keys, values))
    arrived = {0: key_value}
    forward_piece = key_value
    for hop_index in range(1, SPAN + 1):
        forward_piece = from_behind(forward_piece, "view", -1)
        arrived[hop_index] = forward_piece
    backward_piece = key_value
    for hop_index in range(1, SPAN + 1):
        backward_piece = from_behind(backward_piece, "view", 1)
        arrived[-hop_index] = backward_piece
    stacked = jnp.concatenate([arrived[offset] for offset in range(-SPAN, SPAN + 1)], axis=1)
    key_all = stacked[0].reshape(-1, H, head_dim)
    value_all = stacked[1].reshape(-1, H, head_dim)
    query_heads = query.reshape(tokens, H, head_dim)
    grad_heads = grad_out.reshape(tokens, H, head_dim)
    mask_full = mask_spans_of(margin, position, SPAN)
    allowed = block_allowed(mask_full, BLK)
    scores = (
        jnp.einsum("qhd,khd->hqk", query_heads, key_all, preferred_element_type=jnp.float32)
        * score_scale
    )
    scores = jnp.where(allowed[None], scores, NEG_FILL)
    row_max = jnp.max(scores, axis=-1, keepdims=True)
    log_total = row_max + jnp.log(jnp.sum(jnp.exp(scores - row_max), axis=-1, keepdims=True))
    prob_full = jnp.exp(scores - log_total)
    prob_half = prob_full.astype(jnp.bfloat16)
    attended = jnp.einsum(
        "hqk,khd->qhd", prob_half, value_all, preferred_element_type=jnp.float32
    ).astype(jnp.bfloat16)
    row_dot = jnp.sum(grad_heads.astype(jnp.float32) * attended.astype(jnp.float32), axis=-1)
    row_dot = jnp.transpose(row_dot)[..., None]
    prob_grad = jnp.einsum(
        "qhd,khd->hqk", grad_heads, value_all, preferred_element_type=jnp.float32
    )
    grad_half = (prob_full * (prob_grad - row_dot)).astype(jnp.bfloat16)
    grad_query = (
        jnp.einsum("hqk,khd->qhd", grad_half, key_all, preferred_element_type=jnp.float32)
        * score_scale
    )
    grad_query = grad_query.astype(jnp.bfloat16).reshape(tokens, row_width)

    def pair_terms(pair_index):
        start = pair_index * tokens
        grad_cols = grad_half[:, :, start : start + tokens]
        prob_cols = prob_half[:, :, start : start + tokens]
        key_part = jnp.einsum(
            "hqk,qhd->khd", grad_cols, query_heads, preferred_element_type=jnp.float32
        )
        value_part = jnp.einsum(
            "hqk,qhd->khd", prob_cols, grad_heads, preferred_element_type=jnp.float32
        )
        return jnp.stack((key_part, value_part)).reshape(2, tokens, row_width)

    terms = {}
    for offset in range(-SPAN, SPAN + 1):
        if offset == 0:
            terms[offset] = pair_terms(SPAN)
        else:
            terms[offset] = pair_terms(offset + SPAN)
    upward = terms[SPAN]
    for hop_index in range(1, SPAN + 1):
        upward = from_behind(upward, "view", 1)
        if hop_index < SPAN:
            upward = upward + terms[SPAN - hop_index]
    downward = terms[-SPAN]
    for hop_index in range(1, SPAN + 1):
        downward = from_behind(downward, "view", -1)
        if hop_index < SPAN:
            downward = downward + terms[hop_index - SPAN]
    totals = terms[0] + upward + downward
    grad_key = (totals[0] * score_scale).astype(jnp.bfloat16)
    grad_value = totals[1].astype(jnp.bfloat16)
    return (attended.reshape(tokens, row_width), grad_query, grad_key, grad_value)


def solution(mesh):
    return jax.shard_map(
        body,
        mesh=mesh,
        in_specs=(
            P(("groups", "view"), None),
            P(("groups", "view"), None),
            P(("groups", "view"), None),
            P(("groups", "view"), None),
            P("groups", None, None, None),
        ),
        out_specs=(
            P(("groups", "view"), None),
            P(("groups", "view"), None),
            P(("groups", "view"), None),
            P(("groups", "view"), None),
        ),
        check_vma=False,
    )
```

profile of v0, /device:TPU:1, one launch (start us, length us, event | category | flops | bytes accessed | tf_op | source)
XLA Modules:
  0.0 107.7 jit_solution(15547164735799285519)
XLA Ops:
  0.7 1.2 %copy.44 = bf16[128,1024]{0,1:T(8,128)(2,1)S(1)} copy(bf16[128,1024]{1,0:T(8,128)(2,1)} %param.6) | data formatting | bytes 524288 | tf_op args[1]
  1.8 1.1 %copy.45 = bf16[128,1024]{0,1:T(8,128)(2,1)S(1)} copy(bf16[128,1024]{1,0:T(8,128)(2,1)} %param.7) | data formatting | bytes 524288 | tf_op args[2]
  3.0 2.7 %collective-permute-start = (bf16[2,128,1024]{1,2,0:T(8,128)(2,1)S(1)}, bf16[2,128,1024]{1,2,0:T(8,128)(2,1)S(1)}, u32[]{:S(2)}, u32[]{:S(2)}) collective-permute-start(bf16[2,128,1024]{1,2,0:T(8,128)(2,1)S(1)} %pad_maximum_fusion.2), channel_id=1, source_target_pairs={{15,0},{0,1},{1,2},{2,3},{3,4},{4,5},{5,6},{6,7},{7,8},{8,9},{9,10... | collective-permute-start | bytes 1572872 | tf_op jit(solution)/shard_map/ppermute | solution.py:19
  5.7 11.7 %collective-permute-done = bf16[2,128,1024]{1,2,0:T(8,128)(2,1)S(1)} collective-permute-done((bf16[2,128,1024]{1,2,0:T(8,128)(2,1)S(1)}, bf16[2,128,1024]{1,2,0:T(8,128)(2,1)S(1)}, u32[]{:S(2)}, u32[]{:S(2)}) %collective-permute-start) | collective-permute-done | bytes 524320 | tf_op jit(solution)/shard_map/ppermute | solution.py:19
  17.4 2.5 %collective-permute-start.1 = (bf16[2,128,1024]{1,2,0:T(8,128)(2,1)S(1)}, bf16[2,128,1024]{1,2,0:T(8,128)(2,1)S(1)}, u32[]{:S(2)}, u32[]{:S(2)}) collective-permute-start(bf16[2,128,1024]{1,2,0:T(8,128)(2,1)S(1)} %collective-permute-done), channel_id=1, source_target_pairs={{15,0},{0,1},{1,2},{2,3},{3,4},{4,5},{5,6},{6,7},{7,8},{8,9},{9,10... | collective-permute-start | bytes 1572872 | tf_op jit(solution)/shard_map/ppermute | solution.py:19
  20.5 1.1 %copy.95 = bf16[128,1024]{0,1:T(8,128)(2,1)S(1)} copy(bf16[128,1024]{1,0:T(8,128)(2,1)} %param.5) | data formatting | bytes 524288 | tf_op jit(solution)/shard_map/reshape | solution.py:53
  21.6 9.6 %collective-permute-done.1 = bf16[2,128,1024]{1,2,0:T(8,128)(2,1)S(1)} collective-permute-done((bf16[2,128,1024]{1,2,0:T(8,128)(2,1)S(1)}, bf16[2,128,1024]{1,2,0:T(8,128)(2,1)S(1)}, u32[]{:S(2)}, u32[]{:S(2)}) %collective-permute-start.1) | collective-permute-done | bytes 524320 | tf_op jit(solution)/shard_map/ppermute | solution.py:19
  35.1 1.2 %fusion.16 = f32[8,128,128]{1,2,0:T(8,128)} fusion(bf16[128,8,128]{0,2,1:T(8,128)(2,1)S(1)} %bitcast.98, bf16[8,128,640]{1,2,0:T(8,128)(2,1)S(1)} %fusion), kind=kOutput, calls=%fused_computation.32 | convolution fusion | flops 33554432 | bytes 1048576 | tf_op jit(solution)/shard_map/hqk,qhd->khd/dot_general | solution.py:85
  36.3 1.1 %fusion.24 = f32[8,128,128]{1,2,0:T(8,128)} fusion(bf16[128,8,128]{0,2,1:T(8,128)(2,1)S(1)} %bitcast.99, bf16[8,128,640]{1,2,0:T(8,128)(2,1)S(1)} %fusion), kind=kOutput, calls=%fused_computation.40 | convolution fusion | flops 33554432 | bytes 1048576 | tf_op jit(solution)/shard_map/hqk,qhd->khd/dot_general | solution.py:85
  39.6 2.0 %copy.71 = f32[1,128,1024]{2,1,0:T(8,128)} copy(f32[1,128,1024]{1,2,0:T(8,128)} %bitcast.114) | data formatting | bytes 1048576 | tf_op jit(solution)/shard_map/stack | solution.py:91
  41.7 2.0 %copy.61 = f32[1,128,1024]{2,1,0:T(8,128)} copy(f32[1,128,1024]{1,2,0:T(8,128)} %bitcast.113) | data formatting | bytes 1048576 | tf_op jit(solution)/shard_map/stack | solution.py:91
  43.7 2.1 %copy.72 = f32[1,128,1024]{2,1,0:T(8,128)} copy(f32[1,128,1024]{1,2,0:T(8,128)} %bitcast.112) | data formatting | bytes 1048576 | tf_op jit(solution)/shard_map/stack | solution.py:91
  45.8 2.0 %copy.62 = f32[1,128,1024]{2,1,0:T(8,128)} copy(f32[1,128,1024]{1,2,0:T(8,128)} %bitcast.111) | data formatting | bytes 1048576 | tf_op jit(solution)/shard_map/stack | solution.py:91
  47.8 2.4 %pad_maximum_fusion = f32[2,128,1024]{2,1,0:T(8,128)} fusion(f32[1,128,1024]{2,1,0:T(8,128)} %copy.62, f32[1,128,1024]{2,1,0:T(8,128)} %copy.61), kind=kLoop, calls=%fused_computation.15 | loop fusion | flops 262144 | bytes 2097152 | tf_op jit(solution)/shard_map/stack | solution.py:91
  50.2 2.4 %collective-permute-start.4 = (f32[2,128,1024]{2,1,0:T(8,128)}, f32[2,128,1024]{2,1,0:T(8,128)}, u32[]{:S(2)}, u32[]{:S(2)}) collective-permute-start(f32[2,128,1024]{2,1,0:T(8,128)} %pad_maximum_fusion), channel_id=1, source_target_pairs={{15,0},{0,1},{1,2},{2,3},{3,4},{4,5},{5,6},{6,7},{7,8},{8,9},{9,10... | collective-permute-start | bytes 3145736 | tf_op jit(solution)/shard_map/ppermute | solution.py:19
  53.7 2.1 %fusion.12 = f32[8,128,128]{1,2,0:T(8,128)} fusion(bf16[128,8,128]{0,2,1:T(8,128)(2,1)S(1)} %bitcast.100, bf16[8,128,640]{1,2,0:T(8,128)(2,1)} %copy-done), kind=kOutput, calls=%fused_computation.28 | convolution fusion | flops 33554432 | bytes 1048576 | tf_op jit(solution)/shard_map/hqk,qhd->khd/dot_general | solution.py:85
  55.8 2.1 %copy.76 = f32[1,128,1024]{2,1,0:T(8,128)} copy(f32[1,128,1024]{1,2,0:T(8,128)} %bitcast.117) | data formatting | bytes 1048576 | tf_op jit(solution)/shard_map/stack | solution.py:91
  57.9 2.1 %fusion.20 = f32[8,128,128]{1,2,0:T(8,128)} fusion(bf16[128,8,128]{0,2,1:T(8,128)(2,1)S(1)} %bitcast.101, bf16[8,128,640]{1,2,0:T(8,128)(2,1)} %copy-done), kind=kOutput, calls=%fused_computation.36 | convolution fusion | flops 33554432 | bytes 1048576 | tf_op jit(solution)/shard_map/hqk,qhd->khd/dot_general | solution.py:85
  59.9 2.0 %copy.66 = f32[1,128,1024]{2,1,0:T(8,128)} copy(f32[1,128,1024]{1,2,0:T(8,128)} %bitcast.118) | data formatting | bytes 1048576 | tf_op jit(solution)/shard_map/stack | solution.py:91
  62.0 1.1 %fusion.10 = f32[8,128,128]{1,2,0:T(8,128)} fusion(bf16[128,8,128]{0,2,1:T(8,128)(2,1)S(1)} %bitcast.94, bf16[8,128,640]{1,2,0:T(8,128)(2,1)S(1)} %fusion.4), kind=kOutput, calls=%fused_computation.26 | convolution fusion | flops 33554432 | bytes 1048576 | tf_op jit(solution)/shard_map/hqk,qhd->khd/dot_general | solution.py:88
  63.1 2.1 %copy.77 = f32[1,128,1024]{2,1,0:T(8,128)} copy(f32[1,128,1024]{1,2,0:T(8,128)} %bitcast.119) | data formatting | bytes 1048576 | tf_op jit(solution)/shard_map/stack | solution.py:91
  65.1 1.1 %fusion.18 = f32[8,128,128]{1,2,0:T(8,128)} fusion(bf16[128,8,128]{0,2,1:T(8,128)(2,1)S(1)} %bitcast.95, bf16[8,128,640]{1,2,0:T(8,128)(2,1)S(1)} %fusion.4), kind=kOutput, calls=%fused_computation.34 | convolution fusion | flops 33554432 | bytes 1048576 | tf_op jit(solution)/shard_map/hqk,qhd->khd/dot_general | solution.py:88
  66.2 2.0 %copy.67 = f32[1,128,1024]{2,1,0:T(8,128)} copy(f32[1,128,1024]{1,2,0:T(8,128)} %bitcast.120) | data formatting | bytes 1048576 | tf_op jit(solution)/shard_map/stack | solution.py:91
  68.3 7.7 %collective-permute-done.4 = f32[2,128,1024]{2,1,0:T(8,128)} collective-permute-done((f32[2,128,1024]{2,1,0:T(8,128)}, f32[2,128,1024]{2,1,0:T(8,128)}, u32[]{:S(2)}, u32[]{:S(2)}) %collective-permute-start.4) | collective-permute-done | bytes 1048608 | tf_op jit(solution)/shard_map/ppermute | solution.py:19
  75.9 2.7 %maximum_add_fusion.1 = f32[2,128,1024]{2,1,0:T(8,128)} fusion(f32[2,128,1024]{2,1,0:T(8,128)} %collective-permute-done.4, f32[1,128,1024]{2,1,0:T(8,128)} %copy.67, f32[1,128,1024]{2,1,0:T(8,128)} %copy.66), kind=kLoop, calls=%fused_computation.16 | loop fusion | flops 524288 | bytes 3145728 | tf_op jit(solution)/shard_map/add | solution.py:103
  78.6 2.5 %collective-permute-start.5 = (f32[2,128,1024]{2,1,0:T(8,128)}, f32[2,128,1024]{2,1,0:T(8,128)}, u32[]{:S(2)}, u32[]{:S(2)}) collective-permute-start(f32[2,128,1024]{2,1,0:T(8,128)} %maximum_add_fusion.1), channel_id=1, source_target_pairs={{15,0},{0,1},{1,2},{2,3},{3,4},{4,5},{5,6},{6,7},{7,8},{8,9},{9,10... | collective-permute-start | bytes 3145736 | tf_op jit(solution)/shard_map/ppermute | solution.py:19
  81.1 2.3 %maximum_add_fusion.2 = f32[2,128,1024]{2,1,0:T(8,128)} fusion(f32[2,128,1024]{2,1,0:T(8,128)} %collective-permute-done.6, f32[1,128,1024]{2,1,0:T(8,128)S(1)} %copy-done.3, f32[1,128,1024]{2,1,0:T(8,128)S(1)} %copy-done.2), kind=kLoop, calls=%fused_computation.18 | loop fusion | flops 524288 | bytes 3145728 | tf_op jit(solution)/shard_map/add | solution.py:108
  83.4 1.2 %fusion.5 = bf16[8,128,128]{2,1,0:T(8,128)(2,1)} fusion(bf16[640,8,128]{0,2,1:T(8,128)(2,1)S(1)} %bitcast.104, bf16[8,128,640]{1,2,0:T(8,128)(2,1)S(1)} %copy-done.1), kind=kOutput, calls=%fused_computation.12 | convolution fusion | flops 168034304 | bytes 2883584 | tf_op jit(solution)/shard_map/hqk,khd->qhd/dot_general | solution.py:76
  84.6 1.8 %copy.79 = bf16[128,1024]{1,0:T(8,128)(2,1)} copy(bf16[128,1024]{0,1:T(8,128)(2,1)} %bitcast.122) | data formatting | bytes 524288
  87.3 1.2 %fusion.28 = f32[8,128,128]{1,2,0:T(8,128)S(1)} fusion(bf16[128,8,128]{0,2,1:T(8,128)(2,1)S(1)} %bitcast.102, bf16[8,128,640]{1,2,0:T(8,128)(2,1)} %copy-done), kind=kOutput, calls=%fused_computation.44 | convolution fusion | flops 33554432 | bytes 1048576 | tf_op jit(solution)/shard_map/hqk,qhd->khd/dot_general | solution.py:85
  89.2 15.1 %collective-permute-done.5 = f32[2,128,1024]{2,1,0:T(8,128)} collective-permute-done((f32[2,128,1024]{2,1,0:T(8,128)}, f32[2,128,1024]{2,1,0:T(8,128)}, u32[]{:S(2)}, u32[]{:S(2)}) %collective-permute-start.5) | collective-permute-done | bytes 1048608 | tf_op jit(solution)/shard_map/ppermute | solution.py:19
  104.4 1.8 %fusion.6 = f32[2,128,1024]{2,1,0:T(8,128)S(1)} fusion(f32[2,128,1024]{2,1,0:T(8,128)} %collective-permute-done.7, f32[2,128,1024]{2,1,0:T(8,128)} %collective-permute-done.5, f32[1,128,1024]{2,1,0:T(8,128)S(1)} %copy.57, f32[1,128,1024]{2,1,0:T(8,128)S(1)} %copy.56), kind=kLoop, calls=%fused_computation.14 | loop fusion | flops 786432 | bytes 4194304 | tf_op jit(solution)/shard_map/add | solution.py:109
  (50 shorter events, 10.8 us)
Async XLA Ops:
  0.6 19.3 %copy-start.7 = (s32[16,4,1,1]{0,3,2,1:T(1,128)S(1)}, s32[16,4,1,1]{0,3,2,1:T(1,128)}, u32[]{:S(2)}) copy-start(s32[16,4,1,1]{0,3,2,1:T(1,128)} %param.9) | copy-start | bytes 772
  0.6 19.7 %copy-start.6 = (bf16[128,1024]{1,0:T(8,128)(2,1)S(1)}, bf16[128,1024]{1,0:T(8,128)(2,1)}, u32[]{:S(2)}) copy-start(bf16[128,1024]{1,0:T(8,128)(2,1)} %param.8) | copy-start | bytes 786436
  3.0 14.4 %collective-permute-start = (bf16[2,128,1024]{1,2,0:T(8,128)(2,1)S(1)}, bf16[2,128,1024]{1,2,0:T(8,128)(2,1)S(1)}, u32[]{:S(2)}, u32[]{:S(2)}) collective-permute-start(bf16[2,128,1024]{1,2,0:T(8,128)(2,1)S(1)} %pad_maximum_fusion.2), channel_id=1, source_target_pairs={{15,0},{0,1},{1,2},{2,3},{3,4},{4,5},{5,6},{6,7},{7,8},{8,9},{9,10... | collective-permute-start | bytes 1572872 | tf_op jit(solution)/shard_map/ppermute | solution.py:19
  5.7 14.5 %collective-permute-start.2 = (bf16[2,128,1024]{1,2,0:T(8,128)(2,1)S(1)}, bf16[2,128,1024]{1,2,0:T(8,128)(2,1)S(1)}, u32[]{:S(2)}, u32[]{:S(2)}) collective-permute-start(bf16[2,128,1024]{1,2,0:T(8,128)(2,1)S(1)} %pad_maximum_fusion.2), channel_id=1, source_target_pairs={{1,0},{2,1},{3,2},{4,3},{5,4},{6,5},{7,6},{8,7},{9,8},{10,9},{11,1... | collective-permute-start | bytes 1572872 | tf_op jit(solution)/shard_map/ppermute | solution.py:19
  17.4 13.8 %collective-permute-start.1 = (bf16[2,128,1024]{1,2,0:T(8,128)(2,1)S(1)}, bf16[2,128,1024]{1,2,0:T(8,128)(2,1)S(1)}, u32[]{:S(2)}, u32[]{:S(2)}) collective-permute-start(bf16[2,128,1024]{1,2,0:T(8,128)(2,1)S(1)} %collective-permute-done), channel_id=1, source_target_pairs={{15,0},{0,1},{1,2},{2,3},{3,4},{4,5},{5,6},{6,7},{7,8},{8,9},{9,10... | collective-permute-start | bytes 1572872 | tf_op jit(solution)/shard_map/ppermute | solution.py:19
  20.2 11.5 %collective-permute-start.3 = (bf16[2,128,1024]{1,2,0:T(8,128)(2,1)S(1)}, bf16[2,128,1024]{1,2,0:T(8,128)(2,1)S(1)}, u32[]{:S(2)}, u32[]{:S(2)}) collective-permute-start(bf16[2,128,1024]{1,2,0:T(8,128)(2,1)S(1)} %collective-permute-done.2), channel_id=1, source_target_pairs={{1,0},{2,1},{3,2},{4,3},{5,4},{6,5},{7,6},{8,7},{9,8},{10,9},{11,1... | collective-permute-start | bytes 1572872 | tf_op jit(solution)/shard_map/ppermute | solution.py:19
  35.1 3.5 %copy-start = (bf16[8,128,640]{1,2,0:T(8,128)(2,1)}, bf16[8,128,640]{1,2,0:T(8,128)(2,1)S(1)}, u32[]{:S(2)}) copy-start(bf16[8,128,640]{1,2,0:T(8,128)(2,1)S(1)} %fusion) | copy-start | bytes 3932164
  47.8 4.8 %copy-start.4 = (f32[1,128,1024]{2,1,0:T(8,128)S(1)}, f32[1,128,1024]{2,1,0:T(8,128)}, u32[]{:S(2)}) copy-start(f32[1,128,1024]{2,1,0:T(8,128)} %copy.71) | copy-start | bytes 1572868
  47.8 4.8 %copy-start.5 = (f32[1,128,1024]{2,1,0:T(8,128)S(1)}, f32[1,128,1024]{2,1,0:T(8,128)}, u32[]{:S(2)}) copy-start(f32[1,128,1024]{2,1,0:T(8,128)} %copy.72) | copy-start | bytes 1572868
  50.2 25.7 %collective-permute-start.4 = (f32[2,128,1024]{2,1,0:T(8,128)}, f32[2,128,1024]{2,1,0:T(8,128)}, u32[]{:S(2)}, u32[]{:S(2)}) collective-permute-start(f32[2,128,1024]{2,1,0:T(8,128)} %pad_maximum_fusion), channel_id=1, source_target_pairs={{15,0},{0,1},{1,2},{2,3},{3,4},{4,5},{5,6},{6,7},{7,8},{8,9},{9,10... | collective-permute-start | bytes 3145736 | tf_op jit(solution)/shard_map/ppermute | solution.py:19
  53.7 27.4 %collective-permute-start.6 = (f32[2,128,1024]{2,1,0:T(8,128)}, f32[2,128,1024]{2,1,0:T(8,128)}, u32[]{:S(2)}, u32[]{:S(2)}) collective-permute-start(f32[2,128,1024]{2,1,0:T(8,128)} %pad_maximum_fusion.1), channel_id=1, source_target_pairs={{1,0},{2,1},{3,2},{4,3},{5,4},{6,5},{7,6},{8,7},{9,8},{10,9},{11,1... | collective-permute-start | bytes 3145736 | tf_op jit(solution)/shard_map/ppermute | solution.py:19
  68.3 12.8 %copy-start.2 = (f32[1,128,1024]{2,1,0:T(8,128)S(1)}, f32[1,128,1024]{2,1,0:T(8,128)}, u32[]{:S(2)}) copy-start(f32[1,128,1024]{2,1,0:T(8,128)} %copy.76) | copy-start | bytes 1572868
  68.3 12.8 %copy-start.3 = (f32[1,128,1024]{2,1,0:T(8,128)S(1)}, f32[1,128,1024]{2,1,0:T(8,128)}, u32[]{:S(2)}) copy-start(f32[1,128,1024]{2,1,0:T(8,128)} %copy.77) | copy-start | bytes 1572868
  78.6 4.8 %copy-start.1 = (bf16[8,128,640]{1,2,0:T(8,128)(2,1)S(1)}, bf16[8,128,640]{1,2,0:T(8,128)(2,1)}, u32[]{:S(2)}) copy-start(bf16[8,128,640]{1,2,0:T(8,128)(2,1)} %copy-done) | copy-start | bytes 3932164
  78.6 25.8 %collective-permute-start.5 = (f32[2,128,1024]{2,1,0:T(8,128)}, f32[2,128,1024]{2,1,0:T(8,128)}, u32[]{:S(2)}, u32[]{:S(2)}) collective-permute-start(f32[2,128,1024]{2,1,0:T(8,128)} %maximum_add_fusion.1), channel_id=1, source_target_pairs={{15,0},{0,1},{1,2},{2,3},{3,4},{4,5},{5,6},{6,7},{7,8},{8,9},{9,10... | collective-permute-start | bytes 3145736 | tf_op jit(solution)/shard_map/ppermute | solution.py:19
  83.4 21.0 %collective-permute-start.7 = (f32[2,128,1024]{2,1,0:T(8,128)}, f32[2,128,1024]{2,1,0:T(8,128)}, u32[]{:S(2)}, u32[]{:S(2)}) collective-permute-start(f32[2,128,1024]{2,1,0:T(8,128)} %maximum_add_fusion.2), channel_id=1, source_target_pairs={{1,0},{2,1},{3,2},{4,3},{5,4},{6,5},{7,6},{8,7},{9,8},{10,9},{11,1... | collective-permute-start | bytes 3145736 | tf_op jit(solution)/shard_map/ppermute | solution.py:19
where the time goes:
time: 109 us; the launch traced here: 108 us
  waiting for transfers between devices  44.2 us (41%)
  local copies, waits for them, and re-layouts  24.7 us (23%)
  matrix products  15.8 us (14%)
  other arithmetic  12 us (11%)
  starting transfers between devices  10.1 us (9%)
    ppermute x8, waiting for transfers between devices, from_behind(): return lax.ppermute(block, axis, route)  44.2 us
    another operation x10, local copies, waits for them, and re-layouts, pair_terms(): return jnp.stack((key_part, value_part)).reshape(2, tokens, row_width)  16.8 us
    ppermute x8, starting transfers between devices, from_behind(): return lax.ppermute(block, axis, route)  10.1 us
    dot_general x5, matrix products, pair_terms(): jnp.einsum('hqk,qhd->khd', grad_cols, query_heads, preferred_element_type...  7.74 us
    unnamed x24, local copies, waits for them, and re-layouts  5.46 us
    dot_general x5, matrix products, pair_terms(): jnp.einsum('hqk,qhd->khd', prob_cols, grad_heads, preferred_element_type=...  4.69 us
    another operation x2, other arithmetic, pair_terms(): return jnp.stack((key_part, value_part)).reshape(2, tokens, row_width)  3.47 us
    add x1, other arithmetic, body(): upward = upward + terms[SPAN - hop_index]  2.67 us
  transfers between devices with their start and end apart: 8, of which 5 were waited for; matrix products, arithmetic and copies ran while one was open for 26% of the time, Pallas kernels for 0%

commit v1 on v0

v1 whole, which is shorter than its diff:
```python
import functools
import math

import jax
import jax.numpy as jnp
from jax import lax
from jax.experimental import pallas as pl
from jax.experimental.pallas import tpu as pltpu
from jax.sharding import PartitionSpec as P

H = 8
NEG = -1e30

NT = (((1,), (1,)), ((), ()))
NN = (((1,), (0,)), ((), ()))


def dot(a, b, dims):
    return lax.dot_general(a, b, dims, preferred_element_type=jnp.float32)


def roles(i):
    core, pair = i % 2, (i // 2) % 2
    d_core = 1 - 2 * core
    d_pair = 2 - 4 * pair
    return d_core, d_pair, -d_pair, -d_core


def move(x, source_of):
    n = lax.axis_size("view")
    return lax.ppermute(x, "view", [(source_of(i) % n, i) for i in range(n)])


def from_core(x):
    return move(x, lambda i: i ^ 1)


def from_pair(x):
    return move(x, lambda i: i ^ 2)


def from_far(x):
    return move(x, lambda i: i + (4 if (i // 2) % 2 else -4))


def flag(margin_ref, place, d):
    reach = margin_ref.shape[0] // 2
    o = jnp.where(d < 0, d + reach, d + reach - 1)
    return jnp.where(margin_ref[o, place] > 0, 0.0, NEG)


def row_kernel(scale, images, pos_ref, margin_ref, q_ref, k_ref, v_ref, g_ref, kc_ref, vc_ref, p_ref, z_ref, n_ref, *rest):
    att_ref, gq_ref, st_ref = rest[-3:]
    i = pos_ref[0]
    bias = [0.0] + [flag(margin_ref, i, d) for d in roles(i)]
    q, g = q_ref[...], g_ref[...]
    t = q.shape[0]
    k = jnp.concatenate([k_ref[...], kc_ref[...], p_ref[0], z_ref[0], n_ref[0]], axis=0)
    v = jnp.concatenate([v_ref[...], vc_ref[...], p_ref[1], z_ref[1], n_ref[1]], axis=0)
    s = dot(q, k, NT)
    s = jnp.concatenate([s[:, j * t : (j + 1) * t] * scale + bias[j] for j in range(5)], axis=1)
    m = jnp.max(s, axis=1, keepdims=True)
    e = jnp.exp(s - m)
    total = jnp.sum(e, axis=1, keepdims=True)
    prob = e * (1.0 / total)
    att = dot(prob.astype(jnp.bfloat16), v, NN).astype(jnp.bfloat16)
    att_ref[...] = att
    row = jnp.sum(g.astype(jnp.float32) * att.astype(jnp.float32), axis=1, keepdims=True)
    pg = dot(g, v, NT)
    gh = (prob * (pg - row)).astype(jnp.bfloat16)
    gq_ref[...] = (dot(gh, k, NN) * scale).astype(jnp.bfloat16)
    log_total = m + jnp.log(total)
    lane = lax.broadcasted_iota(jnp.int32, (t, 128), 1)
    both = jnp.where(lane == 0, log_total, row)
    st_ref[0] = jnp.transpose(both)[:8]


def col_kernel(scale, images, pos_ref, margin_ref, k_ref, v_ref, q_ref, g_ref, qc_ref, gc_ref, p_ref, z_ref, n_ref,
               so_ref, sc_ref, sp_ref, sz_ref, sn_ref, *rest):
    gk_ref, gv_ref = rest[-2:]
    i = pos_ref[0]
    bias = [0.0]
    for d in roles(i):
        place = i + d
        place = jnp.where(place < 0, place + images, jnp.where(place >= images, place - images, place))
        bias.append(flag(margin_ref, place, -d))
    k, v = k_ref[...], v_ref[...]
    q = jnp.concatenate([q_ref[...], qc_ref[...], p_ref[0], z_ref[0], n_ref[0]], axis=0)
    g = jnp.concatenate([g_ref[...], gc_ref[...], p_ref[1], z_ref[1], n_ref[1]], axis=0)
    stats = [r[0] for r in (so_ref, sc_ref, sp_ref, sz_ref, sn_ref)]
    log_total = jnp.concatenate([st[0:1] - b for st, b in zip(stats, bias)], axis=1)
    row = jnp.concatenate([st[1:2] for st in stats], axis=1)
    s = dot(k, q, NT) * scale
    prob = jnp.exp(s - log_total)
    gv_ref[...] = dot(prob.astype(jnp.bfloat16), g, NN).astype(jnp.bfloat16)
    pg = dot(v, g, NT)
    gh = (prob * (pg - row)).astype(jnp.bfloat16)
    gk_ref[...] = (dot(gh, q, NN) * scale).astype(jnp.bfloat16)


SMEM = pl.BlockSpec(memory_space=pltpu.SMEM)
ANY = pl.BlockSpec(memory_space=pl.ANY)


def call(kernel, name, first, heads, tokens, head_dim, whole, pairs, stats, outs, carried, stat_out, pos, margin):
    own = pl.BlockSpec((tokens, head_dim), lambda h: (0, h + first))
    two = pl.BlockSpec((2, tokens, head_dim), lambda h: (0, 0, h))
    stat = pl.BlockSpec((1, 8, tokens), lambda h: (h, 0, 0))
    args = [pos, margin, *whole, *pairs, *stats]
    specs = [SMEM, SMEM] + [own] * len(whole) + [two] * len(pairs) + [stat] * len(stats)
    aliases = {}
    if carried:
        for n, c in enumerate(carried):
            aliases[len(args)] = n
            args.append(c)
            specs.append(ANY)
    shapes = [jax.ShapeDtypeStruct(whole[0].shape, jnp.bfloat16)] * outs
    out_specs = [own] * outs
    if stat_out:
        shapes.append(jax.ShapeDtypeStruct((heads, 8, tokens), jnp.float32))
        out_specs.append(stat)
    cols = 5 * tokens
    return pl.pallas_call(
        kernel,
        name=name,
        grid=(heads,),
        in_specs=specs,
        out_specs=out_specs,
        out_shape=shapes,
        input_output_aliases=aliases,
        compiler_params=pltpu.CompilerParams(vmem_limit_bytes=16 << 20),
        cost_estimate=pl.CostEstimate(
            flops=heads * 8 * tokens * cols * head_dim,
            transcendentals=heads * tokens * cols,
            bytes_accessed=heads * tokens * head_dim * 2 * 14,
        ),
    )(*args)


def body(query, keys, values, grad_out, margin):
    tokens, width = query.shape
    head_dim = width // H
    scale = 1.0 / math.sqrt(head_dim)
    images = margin.shape[0]
    position = lax.axis_index("view")
    pos = position.reshape(1).astype(jnp.int32)
    margin_t = jnp.transpose(margin, (1, 2, 3, 0)).reshape(margin.shape[1], images)
    hand_pair = (position % 2) == ((position // 2) % 2)

    def cut(x, y, first, heads):
        c = slice(first * head_dim, (first + heads) * head_dim)
        return jnp.stack((x[:, c], y[:, c]))

    def spread(piece):
        pair = from_pair(piece)
        far = from_far(pair)
        near = from_core(jnp.where(hand_pair, pair, far))
        return pair, far, near

    def spread_stats(st):
        return (
            from_core(st),
            from_pair(st),
            move(st, lambda i: i + (2 if (i // 2) % 2 else -2)),
            move(st, lambda i: i + (1 if i % 2 else -1)),
        )

    row_groups = ((0, 4), (4, 4))
    col_groups = ((0, 4), (4, 2), (6, 2))
    kv = [spread(cut(keys, values, f, n)) for f, n in row_groups]
    kc, vc = from_core(keys), from_core(values)
    qg = [spread(cut(query, grad_out, f, n)) for f, n in col_groups]
    qc, gc = from_core(query), from_core(grad_out)

    carried = None
    stats = {}
    for (f, n), pieces in zip(row_groups, kv):
        att, gq, st = call(
            functools.partial(row_kernel, scale, images), "rows%d" % f, f, n, tokens, head_dim,
            (query, keys, values, grad_out, kc, vc), pieces, (), 2, carried, True, pos, margin_t,
        )
        carried = (att, gq)
        stats[(f, n)] = (st, *spread_stats(st))

    carried_kv = None
    for (f, n), pieces in zip(col_groups, qg):
        for (rf, rn), st in stats.items():
            if rf <= f < rf + rn:
                mine = tuple(x[f - rf : f - rf + n] for x in st)
        gk, gv = call(
            functools.partial(col_kernel, scale, images), "cols%d" % f, f, n, tokens, head_dim,
            (keys, values, query, grad_out, qc, gc), pieces, mine, 2, carried_kv, False, pos, margin_t,
        )
        carried_kv = (gk, gv)
    return (*carried, *carried_kv)


def solution(mesh):
    rows = P(("groups", "view"), None)
    return jax.shard_map(
        body,
        mesh=mesh,
        in_specs=(rows, rows, rows, rows, P("groups", None, None, None)),
        out_specs=(rows, rows, rows, rows),
        check_vma=False,
    )
```

time: 109 us -> 86.1 us (0.79)
  the two profiles are of different devices: /device:TPU:1 before, /device:TPU:0 now
where the time goes in v1:
time: 86.1 us; the launch traced here: 85.9 us
  waiting for transfers between devices  43.7 us (51%)
  starting transfers between devices  20.3 us (24%)
  Pallas kernels  18.9 us (22%)
  local copies, waits for them, and re-layouts  1.96 us (2%)
    ppermute x27, waiting for transfers between devices, move(): return lax.ppermute(x, 'view', [(source_of(i) % n, i) for i in range(n)])  43.7 us
    ppermute x27, starting transfers between devices, move(): return lax.ppermute(x, 'view', [(source_of(i) % n, i) for i in range(n)])  20.3 us
    pallas_call x5, Pallas kernels, call(): pl.pallas_call(kernel, name=name, grid=(heads,), in_specs=specs, out_spec...  18.9 us
  transfers between devices with their start and end apart: 27, of which 12 were waited for; matrix products, arithmetic and copies ran while one was open for 2% of the time, Pallas kernels for 19%

profile of v1, /device:TPU:0, one launch (start us, length us, event | category | flops | bytes accessed | tf_op | source)
XLA Modules:
  0.0 85.9 jit_solution(4143501349165558956)
XLA Ops:
  0.6 0.6 collective-permute-start
  1.2 1.0 %slice_bitcast_fusion.3 = (bf16[1,128,512]{2,1,0:T(8,128)(2,1)S(1)}, bf16[1,128,512]{2,1,0:T(8,128)(2,1)S(1)}) fusion(bf16[128,1024]{1,0:T(8,128)(2,1)} %k_ref.9), kind=kLoop, calls=%fused_computation.11 | loop fusion | bytes 524288 | tf_op jit(solution)/shard_map/stack | solution.py:152
  2.3 2.6 %collective-permute-start.2 = (bf16[2,128,512]{2,1,0:T(8,128)(2,1)S(1)}, bf16[2,128,512]{2,1,0:T(8,128)(2,1)S(1)}, u32[]{:S(2)}, u32[]{:S(2)}) collective-permute-start(bf16[2,128,512]{2,1,0:T(8,128)(2,1)S(1)} %pad_maximum_fusion), channel_id=1, source_target_pairs={{2,0},{3,1},{0,2},{1,3},{6,4},{7,5},{4,6},{5,7},{10,8},{11,9},{8,1... | collective-permute-start | bytes 786440 | tf_op jit(solution)/shard_map/ppermute | solution.py:31
  5.0 0.8 copy-done.3
  5.9 1.2 %collective-permute-start.10 = (bf16[2,128,256]{2,1,0:T(8,128)(2,1)S(1)}, bf16[2,128,256]{2,1,0:T(8,128)(2,1)S(1)}, u32[]{:S(2)}, u32[]{:S(2)}) collective-permute-start(bf16[2,128,256]{2,1,0:T(8,128)(2,1)S(1)} %pad_maximum_fusion.3), channel_id=1, source_target_pairs={{2,0},{3,1},{0,2},{1,3},{6,4},{7,5},{4,6},{5,7},{10,8},{11,9},{8,1... | collective-permute-start | bytes 393224 | tf_op jit(solution)/shard_map/ppermute | solution.py:31
  7.1 1.0 %collective-permute-start.17 = (bf16[2,128,256]{2,1,0:T(8,128)(2,1)S(1)}, bf16[2,128,256]{2,1,0:T(8,128)(2,1)S(1)}, u32[]{:S(2)}, u32[]{:S(2)}) collective-permute-start(bf16[2,128,256]{2,1,0:T(8,128)(2,1)S(1)} %pad_maximum_fusion.4), channel_id=1, source_target_pairs={{2,0},{3,1},{0,2},{1,3},{6,4},{7,5},{4,6},{5,7},{10,8},{11,9},{8,1... | collective-permute-start | bytes 393224 | tf_op jit(solution)/shard_map/ppermute | solution.py:31
  8.1 12.3 %collective-permute-done.10.p_ref = bf16[2,128,256]{2,1,0:T(8,128)(2,1)S(1)} collective-permute-done((bf16[2,128,256]{2,1,0:T(8,128)(2,1)S(1)}, bf16[2,128,256]{2,1,0:T(8,128)(2,1)S(1)}, u32[]{:S(2)}, u32[]{:S(2)}) %collective-permute-start.10) | collective-permute-done | bytes 131104 | tf_op jit(solution)/shard_map/ppermute | solution.py:31
  20.4 2.1 %collective-permute-start.11 = (bf16[2,128,256]{2,1,0:T(8,128)(2,1)S(1)}, bf16[2,128,256]{2,1,0:T(8,128)(2,1)S(1)}, u32[]{:S(2)}, u32[]{:S(2)}) collective-permute-start(bf16[2,128,256]{2,1,0:T(8,128)(2,1)S(1)} %collective-permute-done.10.p_ref), channel_id=1, source_target_pairs={{12,0},{13,1},{6,2},{7,3},{0,4},{1,5},{10,6},{11,7},{4,8},{5,9},{1... | collective-permute-start | bytes 393224 | tf_op jit(solution)/shard_map/ppermute | solution.py:31
  23.0 3.2 %collective-permute-start.20 = (bf16[2,128,512]{2,1,0:T(8,128)(2,1)S(1)}, bf16[2,128,512]{2,1,0:T(8,128)(2,1)S(1)}, u32[]{:S(2)}, u32[]{:S(2)}) collective-permute-start(bf16[2,128,512]{2,1,0:T(8,128)(2,1)S(1)} %pad_maximum_fusion.2), channel_id=1, source_target_pairs={{2,0},{3,1},{0,2},{1,3},{6,4},{7,5},{4,6},{5,7},{10,8},{11,9},{8,1... | collective-permute-start | bytes 786440 | tf_op jit(solution)/shard_map/ppermute | solution.py:31
  26.4 1.1 %collective-permute-done.11.z_ref = bf16[2,128,256]{2,1,0:T(8,128)(2,1)S(1)} collective-permute-done((bf16[2,128,256]{2,1,0:T(8,128)(2,1)S(1)}, bf16[2,128,256]{2,1,0:T(8,128)(2,1)S(1)}, u32[]{:S(2)}, u32[]{:S(2)}) %collective-permute-start.11) | collective-permute-done | bytes 131104 | tf_op jit(solution)/shard_map/ppermute | solution.py:31
  27.5 0.5 collective-permute-start.6
  28.1 6.3 %collective-permute-done.18.z_ref = bf16[2,128,256]{2,1,0:T(8,128)(2,1)S(1)} collective-permute-done((bf16[2,128,256]{2,1,0:T(8,128)(2,1)S(1)}, bf16[2,128,256]{2,1,0:T(8,128)(2,1)S(1)}, u32[]{:S(2)}, u32[]{:S(2)}) %collective-permute-start.18) | collective-permute-done | bytes 131104 | tf_op jit(solution)/shard_map/ppermute | solution.py:31
  34.5 5.5 %collective-permute-done.6.z_ref = bf16[2,128,512]{2,1,0:T(8,128)(2,1)S(1)} collective-permute-done((bf16[2,128,512]{2,1,0:T(8,128)(2,1)S(1)}, bf16[2,128,512]{2,1,0:T(8,128)(2,1)S(1)}, u32[]{:S(2)}, u32[]{:S(2)}) %collective-permute-start.6) | collective-permute-done | bytes 262176 | tf_op jit(solution)/shard_map/ppermute | solution.py:31
  40.0 5.6 %collective-permute-done.3.z_ref = bf16[2,128,512]{2,1,0:T(8,128)(2,1)S(1)} collective-permute-done((bf16[2,128,512]{2,1,0:T(8,128)(2,1)S(1)}, bf16[2,128,512]{2,1,0:T(8,128)(2,1)S(1)}, u32[]{:S(2)}, u32[]{:S(2)}) %collective-permute-start.3) | collective-permute-done | bytes 262176 | tf_op jit(solution)/shard_map/ppermute | solution.py:31
  45.7 3.2 %collective-permute-done.21.z_ref = bf16[2,128,512]{2,1,0:T(8,128)(2,1)S(1)} collective-permute-done((bf16[2,128,512]{2,1,0:T(8,128)(2,1)S(1)}, bf16[2,128,512]{2,1,0:T(8,128)(2,1)S(1)}, u32[]{:S(2)}, u32[]{:S(2)}) %collective-permute-start.21) | collective-permute-done | bytes 262176 | tf_op jit(solution)/shard_map/ppermute | solution.py:31
  48.9 0.6 collective-permute-start.9
  49.6 5.0 %rows0.1 = (bf16[128,1024]{1,0:T(8,128)(2,1)}, bf16[128,1024]{1,0:T(8,128)(2,1)}, f32[4,8,128]{2,1,0:T(8,128)S(1)}) custom-call(s32[1]{0:T(128)} %bitcast.pos_ref, s32[4,16]{1,0:T(4,128)S(1)} %bitcast.24, bf16[128,1024]{1,0:T(8,128)(2,1)S(1)} %copy-done, bf16[128,1024]{1,0:T(8,128)(2,1)S(1)} %copy-done.1, bf16[128,1024]{1,0:T(8,128)(2,1)S(1)} %copy-done.2, ...), custom_call_target="tpu_custom_call" | custom-call | flops 335544320 | bytes 1835008 | tf_op jit(solution)/shard_map/rows0/pallas_call | solution.py:123
  54.6 5.0 %rows4.1 = (bf16[128,1024]{1,0:T(8,128)(2,1)}, bf16[128,1024]{1,0:T(8,128)(2,1)}, f32[4,8,128]{2,1,0:T(8,128)S(1)}) custom-call(s32[1]{0:T(128)} %bitcast.pos_ref, s32[4,16]{1,0:T(4,128)S(1)} %bitcast.25, bf16[128,1024]{1,0:T(8,128)(2,1)S(1)} %copy-done, bf16[128,1024]{1,0:T(8,128)(2,1)S(1)} %copy-done.1, ...), custom_call_target="tpu_custom_call", output_to_operand_aliasing={{0}: (11, {}), {1}: (12, {})} | custom-call | flops 335544320 | bytes 1835008 | tf_op jit(solution)/shard_map/rows4/pallas_call | solution.py:123
  59.6 0.5 collective-permute-start.13
  60.1 0.8 collective-permute-done.13
  60.9 3.1 %collective-permute-start.15 = (f32[4,8,128]{2,1,0:T(8,128)S(1)}, f32[4,8,128]{2,1,0:T(8,128)S(1)}, u32[]{:S(2)}, u32[]{:S(2)}) collective-permute-start(f32[4,8,128]{2,1,0:T(8,128)S(1)} %get-tuple-element.20), channel_id=1, source_target_pairs={{14,0},{15,1},{4,2},{5,3},{2,4},{3,5},{8,6},{9,7},{6,8},{7,9},{12,... | collective-permute-start | bytes 49160 | tf_op jit(solution)/shard_map/ppermute | solution.py:31
  64.0 1.4 %collective-permute-start.16 = (f32[4,8,128]{2,1,0:T(8,128)S(1)}, f32[4,8,128]{2,1,0:T(8,128)S(1)}, u32[]{:S(2)}, u32[]{:S(2)}) collective-permute-start(f32[4,8,128]{2,1,0:T(8,128)S(1)} %get-tuple-element.20), channel_id=1, source_target_pairs={{15,0},{2,1},{1,2},{4,3},{3,4},{6,5},{5,6},{8,7},{7,8},{10,9},{9,1... | collective-permute-start | bytes 49160 | tf_op jit(solution)/shard_map/ppermute | solution.py:31
  65.4 1.9 %collective-permute-done.15 = f32[4,8,128]{2,1,0:T(8,128)S(1)} collective-permute-done((f32[4,8,128]{2,1,0:T(8,128)S(1)}, f32[4,8,128]{2,1,0:T(8,128)S(1)}, u32[]{:S(2)}, u32[]{:S(2)}) %collective-permute-start.15) | collective-permute-done | bytes 16416 | tf_op jit(solution)/shard_map/ppermute | solution.py:31
  67.4 0.5 collective-permute-start.12
  68.0 1.9 %collective-permute-done.16 = f32[4,8,128]{2,1,0:T(8,128)S(1)} collective-permute-done((f32[4,8,128]{2,1,0:T(8,128)S(1)}, f32[4,8,128]{2,1,0:T(8,128)S(1)}, u32[]{:S(2)}, u32[]{:S(2)}) %collective-permute-start.16) | collective-permute-done | bytes 16416 | tf_op jit(solution)/shard_map/ppermute | solution.py:31
  69.9 1.3 %collective-permute-start.25 = (f32[4,8,128]{2,1,0:T(8,128)S(1)}, f32[4,8,128]{2,1,0:T(8,128)S(1)}, u32[]{:S(2)}, u32[]{:S(2)}) collective-permute-start(f32[4,8,128]{2,1,0:T(8,128)S(1)} %get-tuple-element.21.so_ref), channel_id=1, source_target_pairs={{14,0},{15,1},{4,2},{5,3},{2,4},{3,5},{8,6},{9,7},{6,8},{7,9},{12,... | collective-permute-start | bytes 49160 | tf_op jit(solution)/shard_map/ppermute | solution.py:31
  71.1 1.4 %collective-permute-start.26 = (f32[4,8,128]{2,1,0:T(8,128)S(1)}, f32[4,8,128]{2,1,0:T(8,128)S(1)}, u32[]{:S(2)}, u32[]{:S(2)}) collective-permute-start(f32[4,8,128]{2,1,0:T(8,128)S(1)} %get-tuple-element.21.so_ref), channel_id=1, source_target_pairs={{15,0},{2,1},{1,2},{4,3},{3,4},{6,5},{5,6},{8,7},{7,8},{10,9},{9,1... | collective-permute-start | bytes 49160 | tf_op jit(solution)/shard_map/ppermute | solution.py:31
  72.5 3.8 %collective-permute-done.25.sz_ref = f32[4,8,128]{2,1,0:T(8,128)S(1)} collective-permute-done((f32[4,8,128]{2,1,0:T(8,128)S(1)}, f32[4,8,128]{2,1,0:T(8,128)S(1)}, u32[]{:S(2)}, u32[]{:S(2)}) %collective-permute-start.25) | collective-permute-done | bytes 16416 | tf_op jit(solution)/shard_map/ppermute | solution.py:31
  76.3 0.7 collective-permute-done.26.sn_ref
  77.0 3.9 %cols0.1 = (bf16[128,1024]{1,0:T(8,128)(2,1)}, bf16[128,1024]{1,0:T(8,128)(2,1)}) custom-call(s32[1]{0:T(128)} %bitcast.pos_ref, s32[4,16]{1,0:T(4,128)S(1)} %bitcast.26, bf16[128,1024]{1,0:T(8,128)(2,1)S(1)} %copy-done.1, bf16[128,1024]{1,0:T(8,128)(2,1)S(1)} %copy-done.2, bf16[128,1024]{1,0:T(8,128)(2,1)S(1)} %copy-done, bf16[128,1024]{1,0:T(8,128)(2,1)S(1)} %copy-done.3, ...), custom_call_target="tpu_custom_call" | custom-call | flops 335544320 | bytes 1835008 | tf_op jit(solution)/shard_map/cols0/pallas_call | solution.py:123
  80.9 2.5 %cols4.1 = (bf16[128,1024]{1,0:T(8,128)(2,1)}, bf16[128,1024]{1,0:T(8,128)(2,1)}) custom-call(s32[1]{0:T(128)} %bitcast.pos_ref, s32[4,16]{1,0:T(4,128)S(1)} %bitcast.27, bf16[128,1024]{1,0:T(8,128)(2,1)S(1)} %copy-done.1, bf16[128,1024]{1,0:T(8,128)(2,1)S(1)} %copy-done.2, ...), custom_call_target="tpu_custom_call", output_to_operand_aliasing={{0}: (16, {}), {1}: (17, {})} | custom-call | flops 167772160 | bytes 917504 | tf_op jit(solution)/shard_map/cols4/pallas_call | solution.py:123
  83.4 2.5 %cols6.1 = (bf16[128,1024]{1,0:T(8,128)(2,1)}, bf16[128,1024]{1,0:T(8,128)(2,1)}) custom-call(s32[1]{0:T(128)} %bitcast.pos_ref, s32[4,16]{1,0:T(4,128)S(1)} %bitcast.28, bf16[128,1024]{1,0:T(8,128)(2,1)S(1)} %copy-done.1, bf16[128,1024]{1,0:T(8,128)(2,1)S(1)} %copy-done.2, ...), custom_call_target="tpu_custom_call", output_to_operand_aliasing={{0}: (16, {}), {1}: (17, {})} | custom-call | flops 167772160 | bytes 917504 | tf_op jit(solution)/shard_map/cols6/pallas_call | solution.py:123
  (58 shorter events, 1.5 us)
Async XLA Ops:
  0.6 1.6 %copy-start.2 = (bf16[128,1024]{1,0:T(8,128)(2,1)S(1)}, bf16[128,1024]{1,0:T(8,128)(2,1)}, u32[]{:S(2)}) copy-start(bf16[128,1024]{1,0:T(8,128)(2,1)} %v_ref.9) | copy-start | bytes 786436
  0.6 48.3 %collective-permute-start = (bf16[128,1024]{1,0:T(8,128)(2,1)}, bf16[128,1024]{1,0:T(8,128)(2,1)S(1)}, u32[]{:S(2)}, u32[]{:S(2)}) collective-permute-start(bf16[128,1024]{1,0:T(8,128)(2,1)} %k_ref.9), channel_id=1, source_target_pairs={{1,0},{0,1},{3,2},{2,3},{5,4},{4,5},{7,6},{6,7},{9,8},{8,9},{11,10... | collective-permute-start | bytes 786440 | tf_op jit(solution)/shard_map/ppermute | solution.py:31
  2.3 25.7 %collective-permute-start.2 = (bf16[2,128,512]{2,1,0:T(8,128)(2,1)S(1)}, bf16[2,128,512]{2,1,0:T(8,128)(2,1)S(1)}, u32[]{:S(2)}, u32[]{:S(2)}) collective-permute-start(bf16[2,128,512]{2,1,0:T(8,128)(2,1)S(1)} %pad_maximum_fusion), channel_id=1, source_target_pairs={{2,0},{3,1},{0,2},{1,3},{6,4},{7,5},{4,6},{5,7},{10,8},{11,9},{8,1... | collective-permute-start | bytes 786440 | tf_op jit(solution)/shard_map/ppermute | solution.py:31
  4.8 0.9 %copy-start.3 = (bf16[128,1024]{1,0:T(8,128)(2,1)S(1)}, bf16[128,1024]{1,0:T(8,128)(2,1)}, u32[]{:S(2)}) copy-start(bf16[128,1024]{1,0:T(8,128)(2,1)} %g_ref.9) | copy-start | bytes 786436
  4.9 1.0 %copy-start = (bf16[128,1024]{1,0:T(8,128)(2,1)S(1)}, bf16[128,1024]{1,0:T(8,128)(2,1)}, u32[]{:S(2)}) copy-start(bf16[128,1024]{1,0:T(8,128)(2,1)} %q_ref.9) | copy-start | bytes 786436
  4.9 21.3 %collective-permute-start.5 = (bf16[2,128,512]{2,1,0:T(8,128)(2,1)S(1)}, bf16[2,128,512]{2,1,0:T(8,128)(2,1)S(1)}, u32[]{:S(2)}, u32[]{:S(2)}) collective-permute-start(bf16[2,128,512]{2,1,0:T(8,128)(2,1)S(1)} %pad_maximum_fusion.1), channel_id=1, source_target_pairs={{2,0},{3,1},{0,2},{1,3},{6,4},{7,5},{4,6},{5,7},{10,8},{11,9},{8,1... | collective-permute-start | bytes 786440 | tf_op jit(solution)/shard_map/ppermute | solution.py:31
  5.9 14.5 %collective-permute-start.10 = (bf16[2,128,256]{2,1,0:T(8,128)(2,1)S(1)}, bf16[2,128,256]{2,1,0:T(8,128)(2,1)S(1)}, u32[]{:S(2)}, u32[]{:S(2)}) collective-permute-start(bf16[2,128,256]{2,1,0:T(8,128)(2,1)S(1)} %pad_maximum_fusion.3), channel_id=1, source_target_pairs={{2,0},{3,1},{0,2},{1,3},{6,4},{7,5},{4,6},{5,7},{10,8},{11,9},{8,1... | collective-permute-start | bytes 393224 | tf_op jit(solution)/shard_map/ppermute | solution.py:31
  7.1 15.9 %collective-permute-start.17 = (bf16[2,128,256]{2,1,0:T(8,128)(2,1)S(1)}, bf16[2,128,256]{2,1,0:T(8,128)(2,1)S(1)}, u32[]{:S(2)}, u32[]{:S(2)}) collective-permute-start(bf16[2,128,256]{2,1,0:T(8,128)(2,1)S(1)} %pad_maximum_fusion.4), channel_id=1, source_target_pairs={{2,0},{3,1},{0,2},{1,3},{6,4},{7,5},{4,6},{5,7},{10,8},{11,9},{8,1... | collective-permute-start | bytes 393224 | tf_op jit(solution)/shard_map/ppermute | solution.py:31
  20.4 7.1 %collective-permute-start.11 = (bf16[2,128,256]{2,1,0:T(8,128)(2,1)S(1)}, bf16[2,128,256]{2,1,0:T(8,128)(2,1)S(1)}, u32[]{:S(2)}, u32[]{:S(2)}) collective-permute-start(bf16[2,128,256]{2,1,0:T(8,128)(2,1)S(1)} %collective-permute-done.10.p_ref), channel_id=1, source_target_pairs={{12,0},{13,1},{6,2},{7,3},{0,4},{1,5},{10,6},{11,7},{4,8},{5,9},{1... | collective-permute-start | bytes 393224 | tf_op jit(solution)/shard_map/ppermute | solution.py:31
  23.0 11.4 %collective-permute-start.20 = (bf16[2,128,512]{2,1,0:T(8,128)(2,1)S(1)}, bf16[2,128,512]{2,1,0:T(8,128)(2,1)S(1)}, u32[]{:S(2)}, u32[]{:S(2)}) collective-permute-start(bf16[2,128,512]{2,1,0:T(8,128)(2,1)S(1)} %pad_maximum_fusion.2), channel_id=1, source_target_pairs={{2,0},{3,1},{0,2},{1,3},{6,4},{7,5},{4,6},{5,7},{10,8},{11,9},{8,1... | collective-permute-start | bytes 786440 | tf_op jit(solution)/shard_map/ppermute | solution.py:31
  26.2 8.2 %collective-permute-start.18 = (bf16[2,128,256]{2,1,0:T(8,128)(2,1)S(1)}, bf16[2,128,256]{2,1,0:T(8,128)(2,1)S(1)}, u32[]{:S(2)}, u32[]{:S(2)}) collective-permute-start(bf16[2,128,256]{2,1,0:T(8,128)(2,1)S(1)} %collective-permute-done.17.p_ref), channel_id=1, source_target_pairs={{12,0},{13,1},{6,2},{7,3},{0,4},{1,5},{10,6},{11,7},{4,8},{5,9},{1... | collective-permute-start | bytes 393224 | tf_op jit(solution)/shard_map/ppermute | solution.py:31
  27.5 12.5 %collective-permute-start.6 = (bf16[2,128,512]{2,1,0:T(8,128)(2,1)S(1)}, bf16[2,128,512]{2,1,0:T(8,128)(2,1)S(1)}, u32[]{:S(2)}, u32[]{:S(2)}) collective-permute-start(bf16[2,128,512]{2,1,0:T(8,128)(2,1)S(1)} %collective-permute-done.5.p_ref), channel_id=1, source_target_pairs={{12,0},{13,1},{6,2},{7,3},{0,4},{1,5},{10,6},{11,7},{4,8},{5,9},{1... | collective-permute-start | bytes 786440 | tf_op jit(solution)/shard_map/ppermute | solution.py:31
  28.0 21.5 %collective-permute-start.1 = (bf16[128,1024]{1,0:T(8,128)(2,1)S(1)}, bf16[128,1024]{1,0:T(8,128)(2,1)S(1)}, u32[]{:S(2)}, u32[]{:S(2)}) collective-permute-start(bf16[128,1024]{1,0:T(8,128)(2,1)S(1)} %copy-done.2), channel_id=1, source_target_pairs={{1,0},{0,1},{3,2},{2,3},{5,4},{4,5},{7,6},{6,7},{9,8},{8,9},{11,10... | collective-permute-start | bytes 786440 | tf_op jit(solution)/shard_map/ppermute | solution.py:31
  34.4 11.2 %collective-permute-start.3 = (bf16[2,128,512]{2,1,0:T(8,128)(2,1)S(1)}, bf16[2,128,512]{2,1,0:T(8,128)(2,1)S(1)}, u32[]{:S(2)}, u32[]{:S(2)}) collective-permute-start(bf16[2,128,512]{2,1,0:T(8,128)(2,1)S(1)} %collective-permute-done.2.p_ref), channel_id=1, source_target_pairs={{12,0},{13,1},{6,2},{7,3},{0,4},{1,5},{10,6},{11,7},{4,8},{5,9},{1... | collective-permute-start | bytes 786440 | tf_op jit(solution)/shard_map/ppermute | solution.py:31
  34.4 33.0 %collective-permute-start.8 = (bf16[128,1024]{1,0:T(8,128)(2,1)S(1)}, bf16[128,1024]{1,0:T(8,128)(2,1)S(1)}, u32[]{:S(2)}, u32[]{:S(2)}) collective-permute-start(bf16[128,1024]{1,0:T(8,128)(2,1)S(1)} %copy-done), channel_id=1, source_target_pairs={{1,0},{0,1},{3,2},{2,3},{5,4},{4,5},{7,6},{6,7},{9,8},{8,9},{11,10... | collective-permute-start | bytes 786440 | tf_op jit(solution)/shard_map/ppermute | solution.py:31
  40.0 8.9 %collective-permute-start.21 = (bf16[2,128,512]{2,1,0:T(8,128)(2,1)S(1)}, bf16[2,128,512]{2,1,0:T(8,128)(2,1)S(1)}, u32[]{:S(2)}, u32[]{:S(2)}) collective-permute-start(bf16[2,128,512]{2,1,0:T(8,128)(2,1)S(1)} %collective-permute-done.20.p_ref), channel_id=1, source_target_pairs={{12,0},{13,1},{6,2},{7,3},{0,4},{1,5},{10,6},{11,7},{4,8},{5,9},{1... | collective-permute-start | bytes 786440 | tf_op jit(solution)/shard_map/ppermute | solution.py:31
  45.6 4.0 %collective-permute-start.7 = (bf16[2,128,512]{2,1,0:T(8,128)(2,1)S(1)}, bf16[2,128,512]{2,1,0:T(8,128)(2,1)S(1)}, u32[]{:S(2)}, u32[]{:S(2)}) collective-permute-start(bf16[2,128,512]{2,1,0:T(8,128)(2,1)S(1)} %broadcast_select_fusion.1), channel_id=1, source_target_pairs={{1,0},{0,1},{3,2},{2,3},{5,4},{4,5},{7,6},{6,7},{9,8},{8,9},{11,10... | collective-permute-start | bytes 786440 | tf_op jit(solution)/shard_map/ppermute | solution.py:31
  45.7 3.9 %copy-start.1 = (bf16[128,1024]{1,0:T(8,128)(2,1)S(1)}, bf16[128,1024]{1,0:T(8,128)(2,1)}, u32[]{:S(2)}) copy-start(bf16[128,1024]{1,0:T(8,128)(2,1)} %k_ref.9) | copy-start | bytes 786436
  48.9 5.7 %collective-permute-start.4 = (bf16[2,128,512]{2,1,0:T(8,128)(2,1)S(1)}, bf16[2,128,512]{2,1,0:T(8,128)(2,1)S(1)}, u32[]{:S(2)}, u32[]{:S(2)}) collective-permute-start(bf16[2,128,512]{2,1,0:T(8,128)(2,1)S(1)} %broadcast_select_fusion.2), channel_id=1, source_target_pairs={{1,0},{0,1},{3,2},{2,3},{5,4},{4,5},{7,6},{6,7},{9,8},{8,9},{11,10... | collective-permute-start | bytes 786440 | tf_op jit(solution)/shard_map/ppermute | solution.py:31
  48.9 0.7 copy-start.4
  48.9 19.0 %collective-permute-start.9 = (bf16[128,1024]{1,0:T(8,128)(2,1)S(1)}, bf16[128,1024]{1,0:T(8,128)(2,1)S(1)}, u32[]{:S(2)}, u32[]{:S(2)}) collective-permute-start(bf16[128,1024]{1,0:T(8,128)(2,1)S(1)} %copy-done.3), channel_id=1, source_target_pairs={{1,0},{0,1},{3,2},{2,3},{5,4},{4,5},{7,6},{6,7},{9,8},{8,9},{11,10... | collective-permute-start | bytes 786440 | tf_op jit(solution)/shard_map/ppermute | solution.py:31
  49.5 18.5 %collective-permute-start.22 = (bf16[2,128,512]{2,1,0:T(8,128)(2,1)S(1)}, bf16[2,128,512]{2,1,0:T(8,128)(2,1)S(1)}, u32[]{:S(2)}, u32[]{:S(2)}) collective-permute-start(bf16[2,128,512]{2,1,0:T(8,128)(2,1)S(1)} %broadcast_select_fusion), channel_id=1, source_target_pairs={{1,0},{0,1},{3,2},{2,3},{5,4},{4,5},{7,6},{6,7},{9,8},{8,9},{11,10... | collective-permute-start | bytes 786440 | tf_op jit(solution)/shard_map/ppermute | solution.py:31
  59.6 1.3 %collective-permute-start.13 = (f32[4,8,128]{2,1,0:T(8,128)S(1)}, f32[4,8,128]{2,1,0:T(8,128)S(1)}, u32[]{:S(2)}, u32[]{:S(2)}) collective-permute-start(f32[4,8,128]{2,1,0:T(8,128)S(1)} %get-tuple-element.20), channel_id=1, source_target_pairs={{1,0},{0,1},{3,2},{2,3},{5,4},{4,5},{7,6},{6,7},{9,8},{8,9},{11,10... | collective-permute-start | bytes 49160 | tf_op jit(solution)/shard_map/ppermute | solution.py:31
  60.1 3.9 %collective-permute-start.14 = (f32[4,8,128]{2,1,0:T(8,128)S(1)}, f32[4,8,128]{2,1,0:T(8,128)S(1)}, u32[]{:S(2)}, u32[]{:S(2)}) collective-permute-start(f32[4,8,128]{2,1,0:T(8,128)S(1)} %get-tuple-element.20), channel_id=1, source_target_pairs={{2,0},{3,1},{0,2},{1,3},{6,4},{7,5},{4,6},{5,7},{10,8},{11,9},{8,1... | collective-permute-start | bytes 49160 | tf_op jit(solution)/shard_map/ppermute | solution.py:31
  60.9 6.4 %collective-permute-start.15 = (f32[4,8,128]{2,1,0:T(8,128)S(1)}, f32[4,8,128]{2,1,0:T(8,128)S(1)}, u32[]{:S(2)}, u32[]{:S(2)}) collective-permute-start(f32[4,8,128]{2,1,0:T(8,128)S(1)} %get-tuple-element.20), channel_id=1, source_target_pairs={{14,0},{15,1},{4,2},{5,3},{2,4},{3,5},{8,6},{9,7},{6,8},{7,9},{12,... | collective-permute-start | bytes 49160 | tf_op jit(solution)/shard_map/ppermute | solution.py:31
  64.0 5.9 %collective-permute-start.16 = (f32[4,8,128]{2,1,0:T(8,128)S(1)}, f32[4,8,128]{2,1,0:T(8,128)S(1)}, u32[]{:S(2)}, u32[]{:S(2)}) collective-permute-start(f32[4,8,128]{2,1,0:T(8,128)S(1)} %get-tuple-element.20), channel_id=1, source_target_pairs={{15,0},{2,1},{1,2},{4,3},{3,4},{6,5},{5,6},{8,7},{7,8},{10,9},{9,1... | collective-permute-start | bytes 49160 | tf_op jit(solution)/shard_map/ppermute | solution.py:31
  67.4 3.8 %collective-permute-start.23 = (f32[4,8,128]{2,1,0:T(8,128)S(1)}, f32[4,8,128]{2,1,0:T(8,128)S(1)}, u32[]{:S(2)}, u32[]{:S(2)}) collective-permute-start(f32[4,8,128]{2,1,0:T(8,128)S(1)} %get-tuple-element.21.so_ref), channel_id=1, source_target_pairs={{1,0},{0,1},{3,2},{2,3},{5,4},{4,5},{7,6},{6,7},{9,8},{8,9},{11,10... | collective-permute-start | bytes 49160 | tf_op jit(solution)/shard_map/ppermute | solution.py:31
  67.4 16.0 %collective-permute-start.12 = (bf16[2,128,256]{2,1,0:T(8,128)(2,1)S(1)}, bf16[2,128,256]{2,1,0:T(8,128)(2,1)S(1)}, u32[]{:S(2)}, u32[]{:S(2)}) collective-permute-start(bf16[2,128,256]{2,1,0:T(8,128)(2,1)S(1)} %broadcast_select_fusion.4), channel_id=1, source_target_pairs={{1,0},{0,1},{3,2},{2,3},{5,4},{4,5},{7,6},{6,7},{9,8},{8,9},{11,10... | collective-permute-start | bytes 393224 | tf_op jit(solution)/shard_map/ppermute | solution.py:31
  67.9 13.0 %collective-permute-start.19 = (bf16[2,128,256]{2,1,0:T(8,128)(2,1)S(1)}, bf16[2,128,256]{2,1,0:T(8,128)(2,1)S(1)}, u32[]{:S(2)}, u32[]{:S(2)}) collective-permute-start(bf16[2,128,256]{2,1,0:T(8,128)(2,1)S(1)} %broadcast_select_fusion.3), channel_id=1, source_target_pairs={{1,0},{0,1},{3,2},{2,3},{5,4},{4,5},{7,6},{6,7},{9,8},{8,9},{11,10... | collective-permute-start | bytes 393224 | tf_op jit(solution)/shard_map/ppermute | solution.py:31
  68.0 4.6 %collective-permute-start.24 = (f32[4,8,128]{2,1,0:T(8,128)S(1)}, f32[4,8,128]{2,1,0:T(8,128)S(1)}, u32[]{:S(2)}, u32[]{:S(2)}) collective-permute-start(f32[4,8,128]{2,1,0:T(8,128)S(1)} %get-tuple-element.21.so_ref), channel_id=1, source_target_pairs={{2,0},{3,1},{0,2},{1,3},{6,4},{7,5},{4,6},{5,7},{10,8},{11,9},{8,1... | collective-permute-start | bytes 49160 | tf_op jit(solution)/shard_map/ppermute | solution.py:31
  69.9 6.4 %collective-permute-start.25 = (f32[4,8,128]{2,1,0:T(8,128)S(1)}, f32[4,8,128]{2,1,0:T(8,128)S(1)}, u32[]{:S(2)}, u32[]{:S(2)}) collective-permute-start(f32[4,8,128]{2,1,0:T(8,128)S(1)} %get-tuple-element.21.so_ref), channel_id=1, source_target_pairs={{14,0},{15,1},{4,2},{5,3},{2,4},{3,5},{8,6},{9,7},{6,8},{7,9},{12,... | collective-permute-start | bytes 49160 | tf_op jit(solution)/shard_map/ppermute | solution.py:31
  71.1 5.9 %collective-permute-start.26 = (f32[4,8,128]{2,1,0:T(8,128)S(1)}, f32[4,8,128]{2,1,0:T(8,128)S(1)}, u32[]{:S(2)}, u32[]{:S(2)}) collective-permute-start(f32[4,8,128]{2,1,0:T(8,128)S(1)} %get-tuple-element.21.so_ref), channel_id=1, source_target_pairs={{15,0},{2,1},{1,2},{4,3},{3,4},{6,5},{5,6},{8,7},{7,8},{10,9},{9,1... | collective-permute-start | bytes 49160 | tf_op jit(solution)/shard_map/ppermute | solution.py:31
